TPU v7x, 32 devices: a whole 2x2x4 slice. The times are simulated.
32 devices in a mesh: groups: 2 (over x), ctx: 16 (over z, y, core).
Axes of the slice: x: 2, y: 2, z: 4, core: 2. Of those that a mesh axis runs over, the one named last changes fastest.
Arguments:
- query_input: bfloat16 [32, 1536], P('groups'), parts along dimension 0, may hold values from -20 to 20
- query_gain: bfloat16 [1536], replicated, may hold values from 0.5 to 1.5
- nope_weight: bfloat16 [1536, 4096], P(None, 'ctx'), may hold values from -0.15625 to 0.15625
- rope_weight: bfloat16 [1536, 2048], P(None, 'ctx'), may hold values from -0.15625 to 0.15625
- key_up: bfloat16 [32, 128, 512], P('ctx'), may hold values from -0.5 to 0.5
- value_up: bfloat16 [32, 512, 128], P('ctx'), may hold values from -1 to 1
- out_weight: bfloat16 [4096, 7168], P('ctx'), may hold values from -0.09375 to 0.09375
- cache_latent: bfloat16 [4, 32768, 512], P('groups', 'ctx'), parts along dimension 0, may hold values from -8 to 8
- cache_rope: bfloat16 [4, 64, 32768], P('groups', None, 'ctx'), parts along dimension 0, may hold values from -256 to 256
- cached_length: int32 [4], P('groups'), parts along dimension 0, may hold values from 16384 to 32760, as said below
Outputs:
- attn_out: bfloat16 [32, 7168], P('groups'), parts along dimension 0
There are 2 independent parts, one for each index of `groups`. A program takes and returns all parts, laid end to end along the dimension named above; an argument that names none is the same for every part. Nothing has to cross between parts.
Inputs may be any that keep to these rules, and one draw needn't show every extreme that they name: `cached_length`: in every part one request has exactly 32760, so that its last new token sees the cache's last position.
All inputs are finite; a program needn't handle non-finite values.
Results may differ from a plain program's by a relative error of at most 0.012.
Values may be sent and summed in bfloat16 or wider, within the bound.
A program may use at most 128 MiB of HBM per device.

v0:
```python
import math
import jax
import jax.numpy as jnp
from jax import lax
from jax.sharding import PartitionSpec as P

mscale_yarn = 1.0 + 0.1 * math.log(40.0)
masked_score = -1e30


def attend_heads(
    latent_query, rope_query, cache_latent, cache_rope, cached_length, positions, softmax_scale
):
    row_count, head_count, latent_width = latent_query.shape
    rope_width = rope_query.shape[2]
    requests = cache_latent.shape[0]
    stretch_rows = row_count // requests
    peak_list, sum_list, pool_list = ([], [], [])
    for request in range(requests):
        flat_latent = latent_query[request * stretch_rows : (request + 1) * stretch_rows].reshape(
            stretch_rows * head_count, latent_width
        )
        flat_rope = rope_query[request * stretch_rows : (request + 1) * stretch_rows].reshape(
            stretch_rows * head_count, rope_width
        )
        scores = jnp.einsum(
            "ql,pl->qp", flat_latent, cache_latent[request], preferred_element_type=jnp.float32
        )
        scores = (
            scores + jnp.dot(flat_rope, cache_rope[request], preferred_element_type=jnp.float32)
        ) * softmax_scale
        last_seen = (
            cached_length[request]
            + jnp.arange(stretch_rows * head_count, dtype=jnp.int32) // head_count
        )
        visible = positions[None, :] <= last_seen[:, None]
        scores = jnp.where(visible, scores, masked_score)
        block_peak = jnp.max(scores, axis=1)
        weights = jnp.where(visible, jnp.exp(scores - block_peak[:, None]), 0.0)
        block_sum = jnp.sum(weights, axis=1)
        block_pool = jnp.dot(
            weights.astype(jnp.bfloat16), cache_latent[request], preferred_element_type=jnp.float32
        )
        peak_list.append(block_peak.reshape(stretch_rows, head_count))
        sum_list.append(block_sum.reshape(stretch_rows, head_count))
        pool_list.append(block_pool.reshape(stretch_rows, head_count, latent_width))
    return (
        jnp.concatenate(peak_list, axis=0),
        jnp.concatenate(sum_list, axis=0),
        jnp.concatenate(pool_list, axis=0),
    )


def project_heads(pooled, weight_sum, value_up, out_weight):
    attended = (pooled / weight_sum[:, :, None]).astype(jnp.bfloat16)
    head_values = jnp.einsum(
        "rhl,hlv->rhv", attended, value_up, preferred_element_type=jnp.float32
    ).astype(jnp.bfloat16)
    return jnp.dot(
        head_values.reshape(head_values.shape[0], -1),
        out_weight,
        preferred_element_type=jnp.float32,
    )


def local(
    query_input,
    query_gain,
    nope_weight,
    rope_weight,
    key_up,
    value_up,
    out_weight,
    cache_latent,
    cache_rope,
    cached_length,
):
    head_local = key_up.shape[0]
    nope_width = key_up.shape[1]
    rope_width = rope_weight.shape[1] // head_local
    row_count = query_input.shape[0]
    key_count = cache_latent.shape[1]
    widened = query_input.astype(jnp.float32)
    normed = (
        widened
        * lax.rsqrt(jnp.mean(widened * widened, axis=-1, keepdims=True) + 1e-06)
        * query_gain.astype(jnp.float32)
    ).astype(jnp.bfloat16)
    query_nope = (
        jnp.dot(normed, nope_weight, preferred_element_type=jnp.float32)
        .astype(jnp.bfloat16)
        .reshape(row_count, head_local, nope_width)
    )
    query_rope = (
        jnp.dot(normed, rope_weight, preferred_element_type=jnp.float32)
        .astype(jnp.bfloat16)
        .reshape(row_count, head_local, rope_width)
    )
    query_latent = jnp.einsum(
        "rhn,hnl->rhl", query_nope, key_up, preferred_element_type=jnp.float32
    ).astype(jnp.bfloat16)
    softmax_scale = mscale_yarn * mscale_yarn / math.sqrt(nope_width + rope_width)
    positions = lax.axis_index("ctx") * key_count + jnp.arange(key_count, dtype=jnp.int32)
    every_latent, every_rope = (
        lax.all_gather(query_latent, "ctx", axis=1, tiled=True),
        lax.all_gather(query_rope, "ctx", axis=1, tiled=True),
    )
    block_peak, block_sum, block_pool = attend_heads(
        every_latent, every_rope, cache_latent, cache_rope, cached_length, positions, softmax_scale
    )
    pooled_in = lax.all_to_all(block_pool[None], "ctx", split_axis=2, concat_axis=0, tiled=True)
    peak_in = lax.all_to_all(block_peak[None], "ctx", split_axis=2, concat_axis=0, tiled=True)
    sum_in = lax.all_to_all(block_sum[None], "ctx", split_axis=2, concat_axis=0, tiled=True)
    row_top = jnp.max(peak_in, axis=0)
    factor = jnp.exp(peak_in - row_top[None])
    pooled = jnp.sum(pooled_in * factor[..., None], axis=0)
    weight_sum = jnp.sum(sum_in * factor, axis=0)
    partial_value = project_heads(pooled, weight_sum, value_up, out_weight)
    return lax.psum(partial_value, "ctx").astype(jnp.bfloat16)


def solution(mesh):
    placed = (
        P("groups", None),
        P(),
        P(None, "ctx"),
        P(None, "ctx"),
        P("ctx", None, None),
        P("ctx", None, None),
        P("ctx", None),
        P("groups", "ctx", None),
        P("groups", None, "ctx"),
        P("groups"),
    )
    return jax.shard_map(
        local, mesh=mesh, in_specs=placed, out_specs=P("groups", None), check_vma=False
    )
```

profile of v0, /device:TPU:0, one launch (start us, length us, event | category | flops | bytes accessed | tf_op | source)
XLA Modules:
  0.0 175.1 jit_solution(12115778293265833145)
XLA Ops:
  0.0 1.4 fusion.44
  1.4 0.7 convert_element_type.40
  2.1 0.9 fusion.28
  3.1 1.1 fusion.21
  4.1 1.1 fusion.20
  5.2 24.6 %all_gather.6 = bf16[16,32,512]{2,0,1:T(8,128)(2,1)S(1)} all-gather(bf16[16,2,512]{2,0,1:T(8,128)(2,1)S(1)} %fusion.20), channel_id=1, replica_groups=mesh['groups'=2,'ctx'=16] {'ctx'}, dimensions={1}, use_global_device_ids=true | all-gather | bytes 557056 | tf_op jit(solution)/shard_map/all_gather | solution.py:105
  30.0 0.2 convolution_convert_fusion.3
  30.3 17.8 %all_gather.7 = bf16[16,32,64]{2,0,1:T(8,128)(2,1)S(1)} all-gather(bf16[16,2,64]{2,0,1:T(8,128)(2,1)S(1)} %copy.64), channel_id=1, replica_groups=mesh['groups'=2,'ctx'=16] {'ctx'}, dimensions={1}, use_global_device_ids=true | all-gather | bytes 69632 | tf_op jit(solution)/shard_map/all_gather | solution.py:106
  48.2 2.5 %fusion.6 = f32[256,2048]{1,0:T(8,128)S(1)} fusion(bf16[256,512]{1,0:T(8,128)(2,1)S(1)} %bitcast.80, bf16[2,2048,512]{2,1,0:T(8,128)(2,1)} %param.17), kind=kOutput, calls=%fused_computation.10 | convolution fusion | flops 536870912 | bytes 4456448 | tf_op jit(solution)/shard_map/ql,pl->qp/dot_general | solution.py:26
  50.7 0.3 copy-done.1
  51.0 0.7 fusion.10
  51.8 1.3 broadcast_add_fusion
  53.1 0.6 fusion.46
  53.8 0.6 fusion.45
  54.4 1.0 fusion.16
  55.6 0.7 copy.72
  56.3 3.5 %all-to-all-start.2 = ((f32[1,16,32]{1,0,2:T(1,128)}), f32[1,16,32]{1,0,2:T(1,128)S(1)}, u32[]{:S(2)}, u32[]{:S(2)}) async-start(f32[1,16,32]{1,0,2:T(1,128)} %copy.72), calls=%async_computation.2 | async-start | bytes 32768 | tf_op jit(solution)/shard_map/all_to_all | solution.py:113
  60.0 2.4 %fusion.4 = f32[8,32,512]{2,1,0:T(8,128)S(1)} fusion(bf16[8,32,2048]{2,1,0:T(8,128)(2,1)S(1)} %bitcast.79, bf16[2,2048,512]{2,1,0:T(8,128)(2,1)} %param.17), kind=kOutput, calls=%fused_computation.8 | convolution fusion | flops 536870912 | bytes 3670016 | tf_op jit(solution)/shard_map/dot_general | solution.py:41
  62.4 0.4 copy-done.2
  62.8 0.7 fusion.8
  63.5 0.7 copy.70
  64.2 2.1 %all-to-all-done.2 = f32[1,16,32]{1,0,2:T(1,128)S(1)} async-done(((f32[1,16,32]{1,0,2:T(1,128)}), f32[1,16,32]{1,0,2:T(1,128)S(1)}, u32[]{:S(2)}, u32[]{:S(2)}) %all-to-all-start.2) | async-done | bytes 2080 | tf_op jit(solution)/shard_map/all_to_all | solution.py:113
  66.3 3.9 %all-to-all-start.1 = ((f32[1,16,32]{1,0,2:T(1,128)}), f32[1,16,32]{1,0,2:T(1,128)S(1)}, u32[]{:S(2)}, u32[]{:S(2)}) async-start(f32[1,16,32]{1,0,2:T(1,128)} %copy.70), calls=%async_computation.1 | async-start | bytes 32768 | tf_op jit(solution)/shard_map/all_to_all | solution.py:112
  70.3 1.6 copy.68
  71.9 4.8 %all-to-all-done.1 = f32[1,16,32]{1,0,2:T(1,128)S(1)} async-done(((f32[1,16,32]{1,0,2:T(1,128)}), f32[1,16,32]{1,0,2:T(1,128)S(1)}, u32[]{:S(2)}, u32[]{:S(2)}) %all-to-all-start.1) | async-done | bytes 2080 | tf_op jit(solution)/shard_map/all_to_all | solution.py:112
  76.7 3.7 %all-to-all-start = ((f32[1,16,32,512]{3,1,0,2:T(8,128)}), f32[1,16,32,512]{3,1,0,2:T(8,128)S(1)}, u32[]{:S(2)}, u32[]{:S(2)}) async-start(f32[1,16,32,512]{3,1,0,2:T(8,128)} %copy.68), calls=%async_computation | async-start | bytes 2097152 | tf_op jit(solution)/shard_map/all_to_all | solution.py:111
  80.4 0.2 copy.71
  80.6 22.6 %all-to-all-done = f32[1,16,32,512]{3,1,0,2:T(8,128)S(1)} async-done(((f32[1,16,32,512]{3,1,0,2:T(8,128)}), f32[1,16,32,512]{3,1,0,2:T(8,128)S(1)}, u32[]{:S(2)}, u32[]{:S(2)}) %all-to-all-start) | async-done | bytes 1048608 | tf_op jit(solution)/shard_map/all_to_all | solution.py:111
  103.2 1.1 fusion.23
  104.3 0.2 fusion.22
  104.5 2.6 %fusion.36 = f32[16,7168]{1,0:T(8,128)S(1)} fusion(bf16[256,7168]{1,0:T(8,128)(2,1)} %param.16, bf16[2,2,8,128]{3,2,1,0:T(8,128)(2,1)S(1)} %fusion.22), kind=kOutput, calls=%fused_computation.48 | convolution fusion | flops 58720256 | bytes 4136960 | tf_op jit(solution)/shard_map/dot_general | solution.py:59
  107.1 68.0 %all-reduce.1 = bf16[16,7168]{1,0:T(8,128)(2,1)} all-reduce(f32[16,7168]{1,0:T(8,128)S(1)} %fusion.36), channel_id=1, replica_groups=mesh['groups'=2,'ctx'=16] {'ctx'}, use_global_device_ids=true, to_apply=%region_8.9 | all-reduce | flops 114688 | bytes 688128 | tf_op jit(solution)/shard_map/psum | solution.py:119
  (31 shorter events, 0.8 us)
Async XLA Ops:
  0.0 3.1 %copy-start = (bf16[1536,256]{1,0:T(8,128)(2,1)S(1)}, bf16[1536,256]{1,0:T(8,128)(2,1)}, u32[]{:S(2)}) copy-start(bf16[1536,256]{1,0:T(8,128)(2,1)} %param.12) | copy-start | bytes 2359300
  0.0 30.0 %copy-start.4 = (bf16[16,1536]{1,0:T(8,128)(2,1)S(1)}, bf16[16,1536]{1,0:T(8,128)(2,1)}, u32[]{:S(2)}) copy-start(bf16[16,1536]{1,0:T(8,128)(2,1)} %param.10) | copy-start | bytes 147460
  0.0 30.0 %copy-start.5 = (bf16[1536,128]{1,0:T(8,128)(2,1)S(1)}, bf16[1536,128]{1,0:T(8,128)(2,1)}, u32[]{:S(2)}) copy-start(bf16[1536,128]{1,0:T(8,128)(2,1)} %param.13) | copy-start | bytes 1179652
  48.2 2.8 %copy-start.1 = (bf16[2,2048,512]{2,1,0:T(8,128)(2,1)S(1)}, bf16[2,2048,512]{2,1,0:T(8,128)(2,1)}, u32[]{:S(2)}) copy-start(bf16[2,2048,512]{2,1,0:T(8,128)(2,1)} %param.17) | copy-start | bytes 12582916
  51.0 2.1 %copy-start.3 = (bf16[2,64,2048]{2,1,0:T(8,128)(2,1)S(1)}, bf16[2,64,2048]{2,1,0:T(8,128)(2,1)}, u32[]{:S(2)}) copy-start(bf16[2,64,2048]{2,1,0:T(8,128)(2,1)} %param.18) | copy-start | bytes 1572868
  56.3 10.0 %all-to-all-start.2 = ((f32[1,16,32]{1,0,2:T(1,128)}), f32[1,16,32]{1,0,2:T(1,128)S(1)}, u32[]{:S(2)}, u32[]{:S(2)}) async-start(f32[1,16,32]{1,0,2:T(1,128)} %copy.72), calls=%async_computation.2 | async-start | bytes 32768 | tf_op jit(solution)/shard_map/all_to_all | solution.py:113
  60.0 2.8 %copy-start.2 = (bf16[2,2048,512]{2,1,0:T(8,128)(2,1)S(1)}, bf16[2,2048,512]{2,1,0:T(8,128)(2,1)}, u32[]{:S(2)}) copy-start(bf16[2,2048,512]{2,1,0:T(8,128)(2,1)} %param.17) | copy-start | bytes 12582916
  66.3 10.4 %all-to-all-start.1 = ((f32[1,16,32]{1,0,2:T(1,128)}), f32[1,16,32]{1,0,2:T(1,128)S(1)}, u32[]{:S(2)}, u32[]{:S(2)}) async-start(f32[1,16,32]{1,0,2:T(1,128)} %copy.70), calls=%async_computation.1 | async-start | bytes 32768 | tf_op jit(solution)/shard_map/all_to_all | solution.py:112
  71.9 32.4 %copy-start.6 = (bf16[2,512,128]{2,1,0:T(8,128)(2,1)S(1)}, bf16[2,512,128]{2,1,0:T(8,128)(2,1)}, u32[]{:S(2)}) copy-start(bf16[2,512,128]{2,1,0:T(8,128)(2,1)} %param.15) | copy-start | bytes 786436
  76.7 26.5 %all-to-all-start = ((f32[1,16,32,512]{3,1,0,2:T(8,128)}), f32[1,16,32,512]{3,1,0,2:T(8,128)S(1)}, u32[]{:S(2)}, u32[]{:S(2)}) async-start(f32[1,16,32,512]{3,1,0,2:T(8,128)} %copy.68), calls=%async_computation | async-start | bytes 2097152 | tf_op jit(solution)/shard_map/all_to_all | solution.py:111
where the time goes:
time: 176 us; the launch traced here: 175 us
  blocking collectives  110 us (62%)
  waiting for transfers between devices  29.5 us (17%)
  matrix products  12.8 us (7%)
  starting transfers between devices  11 us (6%)
  local copies, waits for them, and re-layouts  5.92 us (3%)
  other arithmetic  5.27 us (3%)
    psum x1, blocking collectives, local(): return lax.psum(partial_value, 'ctx').astype(jnp.bfloat16)  68 us
    all_gather x1, blocking collectives, local(): lax.all_gather(query_latent, 'ctx', axis=1, tiled=True)  24.6 us
    all_to_all x1, waiting for transfers between devices, local(): lax.all_to_all(block_pool[None], 'ctx', split_axis=2, concat_axis=0, tile...  22.6 us
    all_gather x1, blocking collectives, local(): lax.all_gather(query_rope, 'ctx', axis=1, tiled=True)  17.8 us
    all_to_all x1, waiting for transfers between devices, local(): lax.all_to_all(block_peak[None], 'ctx', split_axis=2, concat_axis=0, tile...  4.8 us
    all_to_all x1, starting transfers between devices, local(): lax.all_to_all(block_peak[None], 'ctx', split_axis=2, concat_axis=0, tile...  3.88 us
    all_to_all x1, starting transfers between devices, local(): lax.all_to_all(block_pool[None], 'ctx', split_axis=2, concat_axis=0, tile...  3.65 us
  transfers between devices with their start and end apart: 3, of which 3 were waited for; matrix products, arithmetic and copies ran while one was open for 3% of the time, Pallas kernels for 0%

commit v1 on v0

--- a/solution.py
+++ b/solution.py
@@ -75,6 +75,12 @@
     cache_rope,
     cached_length,
 ):
+
+    def update_the_goods(state, dev_axis):
+        wide_out = lax.psum(1, dev_axis)
+        near = jnp.stack(jnp.split(state, wide_out, axis=2))
+        return jnp.concatenate(lax.all_to_all(near, dev_axis, 0, 0), axis=0)
+
     head_local = key_up.shape[0]
     nope_width = key_up.shape[1]
     rope_width = rope_weight.shape[1] // head_local
@@ -108,7 +114,7 @@
     block_peak, block_sum, block_pool = attend_heads(
         every_latent, every_rope, cache_latent, cache_rope, cached_length, positions, softmax_scale
     )
-    pooled_in = lax.all_to_all(block_pool[None], "ctx", split_axis=2, concat_axis=0, tiled=True)
+    pooled_in = update_the_goods(block_pool[None], "ctx")
     peak_in = lax.all_to_all(block_peak[None], "ctx", split_axis=2, concat_axis=0, tiled=True)
     sum_in = lax.all_to_all(block_sum[None], "ctx", split_axis=2, concat_axis=0, tiled=True)
     row_top = jnp.max(peak_in, axis=0)

time: 176 us -> 185 us (1.051)
  local copies, waits for them, and re-layouts: 5.92 us -> 14.6 us
  starting transfers between devices: 11 us -> 13.1 us
    unnamed x16 -> x31, local copies, waits for them, and re-layouts: 0.88 us -> 10.6 us
    all_to_all x1, waiting for transfers between devices: 2.1 us -> 0.01 us  [local(): lax.all_to_all(block_sum[None], 'ctx', split_axis=2, concat_axis=0, tiled...]
    all_to_all x1, starting transfers between devices: 3.88 us -> 5.97 us  [local(): lax.all_to_all(block_peak[None], 'ctx', split_axis=2, concat_axis=0, tile...]
  transfers between devices with their start and end apart: 3 -> 3, of which waited for: 3 -> 2; matrix products, arithmetic and copies ran while one was open for 3% -> 8% of each run, Pallas kernels for 0% -> 0%
where the time goes in v1:
time: 185 us; the launch traced here: 184 us
  blocking collectives  110 us (59%)
  waiting for transfers between devices  28.5 us (15%)
  local copies, waits for them, and re-layouts  14.6 us (8%)
  starting transfers between devices  13.1 us (7%)
  matrix products  12.8 us (7%)
  other arithmetic  4.66 us (3%)
    psum x1, blocking collectives, local(): return lax.psum(partial_value, 'ctx').astype(jnp.bfloat16)  68 us
    all_gather x1, blocking collectives, local(): lax.all_gather(query_latent, 'ctx', axis=1, tiled=True)  24.6 us
    all_to_all x1, waiting for transfers between devices, update_the_goods(): return jnp.concatenate(lax.all_to_all(near, dev_axis, 0, 0), axis=0)  22.6 us
    all_gather x1, blocking collectives, local(): lax.all_gather(query_rope, 'ctx', axis=1, tiled=True)  17.8 us
    unnamed x31, local copies, waits for them, and re-layouts  10.6 us
    all_to_all x1, starting transfers between devices, local(): lax.all_to_all(block_peak[None], 'ctx', split_axis=2, concat_axis=0, tile...  5.97 us
    all_to_all x1, waiting for transfers between devices, local(): lax.all_to_all(block_peak[None], 'ctx', split_axis=2, concat_axis=0, tile...  5.84 us
  transfers between devices with their start and end apart: 3, of which 2 were waited for; matrix products, arithmetic and copies ran while one was open for 8% of the time, Pallas kernels for 0%

profile of v1, /device:TPU:0, one launch (start us, length us, event | category | flops | bytes accessed | tf_op | source)
XLA Modules:
  0.0 184.3 jit_solution(543909023371158633)
XLA Ops:
  0.0 1.4 fusion.60
  1.4 0.7 convert_element_type.40
  2.1 0.9 fusion.28
  3.1 1.1 fusion.21
  4.1 1.1 fusion.20
  5.2 24.6 %all_gather.6 = bf16[16,32,512]{2,0,1:T(8,128)(2,1)S(1)} all-gather(bf16[16,2,512]{2,0,1:T(8,128)(2,1)S(1)} %fusion.20), channel_id=1, replica_groups=mesh['groups'=2,'ctx'=16] {'ctx'}, dimensions={1}, use_global_device_ids=true | all-gather | bytes 557056 | tf_op jit(solution)/shard_map/all_gather | solution.py:111
  30.3 17.8 %all_gather.7 = bf16[16,32,64]{2,0,1:T(8,128)(2,1)S(1)} all-gather(bf16[16,2,64]{2,0,1:T(8,128)(2,1)S(1)} %copy.58), channel_id=1, replica_groups=mesh['groups'=2,'ctx'=16] {'ctx'}, dimensions={1}, use_global_device_ids=true | all-gather | bytes 69632 | tf_op jit(solution)/shard_map/all_gather | solution.py:112
  48.2 2.5 %fusion.6 = f32[256,2048]{1,0:T(8,128)S(1)} fusion(bf16[256,512]{1,0:T(8,128)(2,1)S(1)} %bitcast.140, bf16[2,2048,512]{2,1,0:T(8,128)(2,1)} %param.17), kind=kOutput, calls=%fused_computation.10 | convolution fusion | flops 536870912 | bytes 4456448 | tf_op jit(solution)/shard_map/ql,pl->qp/dot_general | solution.py:26
  51.0 0.7 fusion.10
  51.8 1.3 broadcast_add_fusion
  54.4 1.0 fusion.16
  55.6 0.7 copy.64
  56.3 3.5 %all-to-all-start.2 = ((f32[1,16,32]{1,0,2:T(1,128)}), f32[1,16,32]{1,0,2:T(1,128)S(1)}, u32[]{:S(2)}, u32[]{:S(2)}) async-start(f32[1,16,32]{1,0,2:T(1,128)} %copy.64), calls=%async_computation.2 | async-start | bytes 32768 | tf_op jit(solution)/shard_map/all_to_all | solution.py:119
  60.0 2.4 %fusion.4 = f32[8,32,512]{2,1,0:T(8,128)S(1)} fusion(bf16[8,32,2048]{2,1,0:T(8,128)(2,1)S(1)} %bitcast.139, bf16[2,2048,512]{2,1,0:T(8,128)(2,1)} %param.17), kind=kOutput, calls=%fused_computation.8 | convolution fusion | flops 536870912 | bytes 3670016 | tf_op jit(solution)/shard_map/dot_general | solution.py:41
  62.8 0.7 fusion.8
  64.2 0.6 fusion.45
  64.9 0.6 fusion.44
  65.5 0.6 fusion.43
  66.8 0.7 fusion.41
  67.5 0.6 fusion.40
  69.4 0.6 fusion.37
  70.1 0.6 fusion.36
  72.0 0.6 fusion.33
  72.6 0.7 fusion.32
  73.3 0.7 copy.62
  74.0 6.0 %all-to-all-start.1 = ((f32[1,16,32]{1,0,2:T(1,128)}), f32[1,16,32]{1,0,2:T(1,128)S(1)}, u32[]{:S(2)}, u32[]{:S(2)}) async-start(f32[1,16,32]{1,0,2:T(1,128)} %copy.62), calls=%async_computation.1 | async-start | bytes 32768 | tf_op jit(solution)/shard_map/all_to_all | solution.py:118
  79.9 0.7 fusion.31
  80.6 5.8 %all-to-all-done.1 = f32[1,16,32]{1,0,2:T(1,128)S(1)} async-done(((f32[1,16,32]{1,0,2:T(1,128)}), f32[1,16,32]{1,0,2:T(1,128)S(1)}, u32[]{:S(2)}, u32[]{:S(2)}) %all-to-all-start.1) | async-done | bytes 2080 | tf_op jit(solution)/shard_map/all_to_all | solution.py:118
  86.4 3.7 %all-to-all-start = ((f32[16,1,16,2,512]{4,3,2,1,0:T(2,128)}), f32[16,1,16,2,512]{4,3,2,1,0:T(2,128)S(1)}, u32[]{:S(2)}, u32[]{:S(2)}) async-start(f32[16,1,16,2,512]{4,3,2,1,0:T(2,128)} %fusion.31), calls=%async_computation | async-start | bytes 2097152 | tf_op jit(solution)/shard_map/all_to_all | solution.py:82
  90.3 22.6 %all-to-all-done = f32[16,1,16,2,512]{4,3,2,1,0:T(2,128)S(1)} async-done(((f32[16,1,16,2,512]{4,3,2,1,0:T(2,128)}), f32[16,1,16,2,512]{4,3,2,1,0:T(2,128)S(1)}, u32[]{:S(2)}, u32[]{:S(2)}) %all-to-all-start) | async-done | bytes 1048608 | tf_op jit(solution)/shard_map/all_to_all | solution.py:82
  113.7 2.6 %fusion.52 = f32[16,7168]{1,0:T(8,128)S(1)} fusion(bf16[256,7168]{1,0:T(8,128)(2,1)} %param.16, bf16[2,2,8,128]{3,2,1,0:T(8,128)(2,1)S(1)} %fusion.22), kind=kOutput, calls=%fused_computation.80 | convolution fusion | flops 58720256 | bytes 4136960 | tf_op jit(solution)/shard_map/dot_general | solution.py:59
  116.3 68.0 %all-reduce.1 = bf16[16,7168]{1,0:T(8,128)(2,1)} all-reduce(f32[16,7168]{1,0:T(8,128)S(1)} %fusion.52), channel_id=1, replica_groups=mesh['groups'=2,'ctx'=16] {'ctx'}, use_global_device_ids=true, to_apply=%region_8.9 | all-reduce | flops 114688 | bytes 688128 | tf_op jit(solution)/shard_map/psum | solution.py:125
  (46 shorter events, 7.7 us)
Async XLA Ops:
  0.0 3.1 %copy-start = (bf16[1536,256]{1,0:T(8,128)(2,1)S(1)}, bf16[1536,256]{1,0:T(8,128)(2,1)}, u32[]{:S(2)}) copy-start(bf16[1536,256]{1,0:T(8,128)(2,1)} %param.12) | copy-start | bytes 2359300
  0.0 30.0 %copy-start.4 = (bf16[16,1536]{1,0:T(8,128)(2,1)S(1)}, bf16[16,1536]{1,0:T(8,128)(2,1)}, u32[]{:S(2)}) copy-start(bf16[16,1536]{1,0:T(8,128)(2,1)} %param.10) | copy-start | bytes 147460
  0.0 30.0 %copy-start.5 = (bf16[1536,128]{1,0:T(8,128)(2,1)S(1)}, bf16[1536,128]{1,0:T(8,128)(2,1)}, u32[]{:S(2)}) copy-start(bf16[1536,128]{1,0:T(8,128)(2,1)} %param.13) | copy-start | bytes 1179652
  48.2 2.8 %copy-start.1 = (bf16[2,2048,512]{2,1,0:T(8,128)(2,1)S(1)}, bf16[2,2048,512]{2,1,0:T(8,128)(2,1)}, u32[]{:S(2)}) copy-start(bf16[2,2048,512]{2,1,0:T(8,128)(2,1)} %param.17) | copy-start | bytes 12582916
  51.0 2.1 %copy-start.3 = (bf16[2,64,2048]{2,1,0:T(8,128)(2,1)S(1)}, bf16[2,64,2048]{2,1,0:T(8,128)(2,1)}, u32[]{:S(2)}) copy-start(bf16[2,64,2048]{2,1,0:T(8,128)(2,1)} %param.18) | copy-start | bytes 1572868
  56.3 17.6 %all-to-all-start.2 = ((f32[1,16,32]{1,0,2:T(1,128)}), f32[1,16,32]{1,0,2:T(1,128)S(1)}, u32[]{:S(2)}, u32[]{:S(2)}) async-start(f32[1,16,32]{1,0,2:T(1,128)} %copy.64), calls=%async_computation.2 | async-start | bytes 32768 | tf_op jit(solution)/shard_map/all_to_all | solution.py:119
  60.0 2.8 %copy-start.2 = (bf16[2,2048,512]{2,1,0:T(8,128)(2,1)S(1)}, bf16[2,2048,512]{2,1,0:T(8,128)(2,1)}, u32[]{:S(2)}) copy-start(bf16[2,2048,512]{2,1,0:T(8,128)(2,1)} %param.17) | copy-start | bytes 12582916
  71.3 42.1 %copy-start.6 = (bf16[2,512,128]{2,1,0:T(8,128)(2,1)S(1)}, bf16[2,512,128]{2,1,0:T(8,128)(2,1)}, u32[]{:S(2)}) copy-start(bf16[2,512,128]{2,1,0:T(8,128)(2,1)} %param.15) | copy-start | bytes 786436
  74.0 12.5 %all-to-all-start.1 = ((f32[1,16,32]{1,0,2:T(1,128)}), f32[1,16,32]{1,0,2:T(1,128)S(1)}, u32[]{:S(2)}, u32[]{:S(2)}) async-start(f32[1,16,32]{1,0,2:T(1,128)} %copy.62), calls=%async_computation.1 | async-start | bytes 32768 | tf_op jit(solution)/shard_map/all_to_all | solution.py:118
  86.4 26.5 %all-to-all-start = ((f32[16,1,16,2,512]{4,3,2,1,0:T(2,128)}), f32[16,1,16,2,512]{4,3,2,1,0:T(2,128)S(1)}, u32[]{:S(2)}, u32[]{:S(2)}) async-start(f32[16,1,16,2,512]{4,3,2,1,0:T(2,128)} %fusion.31), calls=%async_computation | async-start | bytes 2097152 | tf_op jit(solution)/shard_map/all_to_all | solution.py:82
